TPU v7x, 32 devices: a whole 2x2x4 slice. The times are simulated.
32 devices in a mesh: dp: 8 (over z, core), width: 4 (over y, x).
Axes of the slice: x: 2, y: 2, z: 4, core: 2. Of those that a mesh axis runs over, the one named last changes fastest.
Arguments:
- inputs: bfloat16 [1536, 4, 512], P('dp', 'width'), may hold values from -6 to 6
- block_weights: bfloat16 [4, 512, 3, 512], P('width'), may hold values from -0.15625 to 0.15625
- low_left: bfloat16 [4, 512, 256], P('width'), may hold values from -0.125 to 0.125
- low_right: bfloat16 [4, 256, 512], P('width'), may hold values from -0.375 to 0.375
- out_grad: bfloat16 [1536, 4, 512], P('dp', 'width'), may hold values from -6 to 6
Outputs:
- activations: bfloat16 [1536, 4, 512], P('dp', 'width')
- in_grad: bfloat16 [1536, 4, 512], P('dp', 'width')
- block_grad: float32 [4, 512, 3, 512], P('width', 'dp')
- left_grad: float32 [4, 512, 256], P('width', 'dp')
- right_grad: float32 [4, 256, 512], P('width', 'dp')
All inputs are finite; a program needn't handle non-finite values.
Results may differ from a plain program's by a relative error of at most 0.0061.
Values may be sent and summed in bfloat16 or wider, within the bound.
A program may use at most 64 MiB of HBM per device.

v0:
```python
import math

import jax
import jax.numpy as jnp
from jax import lax
from jax.sharding import PartitionSpec as P

root_half = 0.7071067811865476
inv_root_two_pi = 0.3989422804014327


def swapped(array, axis, apart):
    return lax.ppermute(array, axis, [(i, i ^ 1 << apart) for i in range(lax.axis_size(axis))])


def gelu_value(pre):
    return 0.5 * pre * (1.0 + lax.erf(pre * root_half))


def gelu_slope(pre):
    return (
        0.5 * (1.0 + lax.erf(pre * root_half)) + pre * jnp.exp(-0.5 * pre * pre) * inv_root_two_pi
    )


def shards(inputs, block_weights, low_left, low_right, out_grad):
    own_x = inputs[:, 0]
    weights = block_weights[0]
    left = low_left[0]
    right = low_right[0]
    grad_out = out_grad[:, 0]
    levels = lax.axis_size("width").bit_length() - 1
    block_size = own_x.shape[1]
    scale = 1.0 / math.sqrt(own_x.shape[0] * lax.axis_size("dp"))
    pieces = [own_x]
    for bit in range(levels):
        pieces.append(swapped(own_x, "width", bit))
    all_x = jnp.stack(pieces, axis=1)
    latent = lax.psum(jnp.dot(own_x, left, preferred_element_type=jnp.float32), "width").astype(
        jnp.bfloat16
    )
    pre = lax.dot_general(
        all_x, weights, (((1, 2), (1, 2)), ((), ())), preferred_element_type=jnp.float32
    )
    pre = pre + jnp.dot(latent, right, preferred_element_type=jnp.float32)
    activations = gelu_value(pre).astype(jnp.bfloat16)
    hidden = (grad_out.astype(jnp.float32) * gelu_slope(pre)).astype(jnp.bfloat16)
    latent_term = lax.dot_general(
        hidden, right, (((1,), (1,)), ((), ())), preferred_element_type=jnp.float32
    )
    latent_grad = lax.psum(latent_term, "width").astype(jnp.bfloat16)
    partner_w = weights[:, 1:, :].reshape(weights.shape[0], levels * block_size)
    backs = jnp.dot(hidden, partner_w, preferred_element_type=jnp.float32).astype(jnp.bfloat16)
    returned = jnp.zeros(own_x.shape, jnp.float32)
    for bit in range(levels):
        piece = backs[:, bit * block_size : (bit + 1) * block_size]
        returned = returned + swapped(piece, "width", bit).astype(jnp.float32)
    own_back = jnp.dot(hidden, weights[:, 0, :], preferred_element_type=jnp.float32)
    own_back = own_back + lax.dot_general(
        latent_grad, left, (((1,), (1,)), ((), ())), preferred_element_type=jnp.float32
    )
    in_grad = (own_back + returned).astype(jnp.bfloat16)
    left_term = (
        lax.dot_general(
            own_x, latent_grad, (((0,), (0,)), ((), ())), preferred_element_type=jnp.float32
        )
        * scale
    )
    right_term = (
        lax.dot_general(
            latent, hidden, (((0,), (0,)), ((), ())), preferred_element_type=jnp.float32
        )
        * scale
    )
    block_term = (
        lax.dot_general(hidden, all_x, (((0,), (0,)), ((), ())), preferred_element_type=jnp.float32)
        * scale
    )
    block_grad, left_grad, right_grad = (
        lax.psum_scatter(block_term, "dp", scatter_dimension=0, tiled=True),
        lax.psum_scatter(left_term, "dp", scatter_dimension=0, tiled=True),
        lax.psum_scatter(right_term, "dp", scatter_dimension=0, tiled=True),
    )
    return (
        activations[:, None],
        in_grad[:, None],
        block_grad[None],
        left_grad[None],
        right_grad[None],
    )


def solution(mesh):
    placed = (
        P("dp", "width", None),
        P("width", None, None, None),
        P("width", None, None),
        P("width", None, None),
        P("dp", "width", None),
    )
    return jax.shard_map(
        shards,
        mesh=mesh,
        in_specs=placed,
        out_specs=(
            P("dp", "width", None),
            P("dp", "width", None),
            P("width", "dp", None, None),
            P("width", "dp", None),
            P("width", "dp", None),
        ),
        check_vma=False,
    )
```

profile of v0, /device:TPU:0, one launch (start us, length us, event | category | flops | bytes accessed | tf_op | source)
XLA Modules:
  0.0 165.7 jit_solution(3442225365040632278)
XLA Ops:
  7.2 0.0 copy-start
  7.2 0.0 copy-start.1
  7.2 0.0 copy-start.3
  7.2 0.0 reduce-scatter.10.cloned.1.call-start
  7.2 3.1 %collective-permute-start.1 = (bf16[192,512]{1,0:T(8,128)(2,1)}, bf16[192,512]{1,0:T(8,128)(2,1)S(1)}, u32[]{:S(2)}, u32[]{:S(2)}) collective-permute-start(bf16[192,512]{1,0:T(8,128)(2,1)} %bitcast.69), channel_id=1, source_target_pairs={{0,2},{1,3},{2,0},{3,1},{4,6},{5,7},{6,4},{7,5},{8,10},{9,11},{10,... | collective-permute-start | bytes 589832 | tf_op jit(solution)/shard_map/ppermute | solution.py:13
  10.3 1.5 collective-permute-start
  11.8 1.3 fusion.21
  13.1 18.4 %all-reduce.2 = bf16[192,256]{1,0:T(8,128)(2,1)S(1)} all-reduce(f32[192,256]{1,0:T(8,128)S(1)} %fusion.21), channel_id=1, replica_groups=mesh['dp'=8,'width'=4] {'width'}, use_global_device_ids=true, to_apply=%region_0.0 | all-reduce | flops 49152 | bytes 294912 | tf_op jit(solution)/shard_map/psum | solution.py:39
  31.5 0.0 copy-done
  31.5 0.2 fusion.18
  31.7 0.0 collective-permute-done.1
  31.7 0.0 collective-permute-done
  31.7 0.0 copy-done.1
  31.7 0.0 copy-done.3
  31.7 2.9 %fusion.15 = (bf16[192,512]{1,0:T(8,128)(2,1)S(1)}, bf16[192,1,512]{2,0,1:T(8,128)(2,1)}) fusion(bf16[192,1,512]{2,0,1:T(8,128)(2,1)S(1)} %copy-done.3, f32[192,512]{1,0:T(8,128)S(1)} %fusion.18, bf16[1,512,3,512]{3,1,2,0:T(8,128)(2,1)} %param.6, bf16[192,1,512]{2,0,1:T(8,128)(2,1)S(1)} %bitcast.72, bf16[192,1,512]{2,0,1:T(8,128)(2,1)S(1)} %bitcast.74, ...), kind=kOutput, calls=%fused_computation.19 | convolution fusion | flops 304054272 | bytes 3145728 | tf_op jit(solution)/shard_map/dot_general | solution.py:42
  34.7 0.2 fusion.16
  34.9 17.6 %all-reduce.3 = bf16[192,256]{1,0:T(8,128)(2,1)S(1)} all-reduce(f32[192,256]{1,0:T(8,128)S(1)} %fusion.16), channel_id=1, replica_groups=mesh['dp'=8,'width'=4] {'width'}, use_global_device_ids=true, to_apply=%region_1.0 | all-reduce | flops 49152 | bytes 294912 | tf_op jit(solution)/shard_map/psum | solution.py:51
  52.6 0.2 fusion.2
  52.8 1.0 copy.20
  53.8 0.0 reduce-scatter.10.cloned.1.call-update
  53.8 0.0 reduce-scatter.8.cloned.1.call-start
  53.9 1.0 convolution_multiply_fusion.1
  54.9 0.0 reduce-scatter.8.cloned.1.call-update
  54.9 0.0 reduce-scatter.6.cloned.1.call-start
  55.0 2.3 %convolution_multiply_fusion = f32[512,3,512]{2,0,1:T(8,128)} fusion(bf16[192,1,512]{2,0,1:T(8,128)(2,1)S(1)} %bitcast.73, bf16[192,1,512]{2,0,1:T(8,128)(2,1)S(1)} %bitcast.75, bf16[192,1,512]{2,0,1:T(8,128)(2,1)S(1)} %copy-done.1, bf16[192,512]{1,0:T(8,128)(2,1)S(1)} %get-tuple-element.22), kind=kOutput, calls=%fused_computation | convolution fusion | flops 304545792 | bytes 3932160 | tf_op jit(solution)/shard_map/dot_general | solution.py:76
  57.2 0.0 reduce-scatter.6.cloned.1.call-update
  57.3 1.7 %copy.14 = bf16[1,512,3,512]{1,3,2,0:T(8,128)(2,1)S(1)} copy(bf16[1,512,3,512]{3,1,2,0:T(8,128)(2,1)} %param.6) | data formatting | bytes 3145728 | tf_op args[1]
  59.0 0.1 slice.17
  59.1 0.0 copy-start.2
  59.1 0.5 convolution_convert_fusion
  59.6 1.2 collective-permute-start.2
  60.8 0.9 collective-permute-start.3
  61.7 0.3 fusion.9
  62.0 3.3 %collective-permute-done.2 = bf16[192,512]{1,0:T(8,128)(2,1)S(1)} collective-permute-done((bf16[192,512]{1,0:T(8,128)(2,1)S(1)}, bf16[192,512]{1,0:T(8,128)(2,1)S(1)}, u32[]{:S(2)}, u32[]{:S(2)}) %collective-permute-start.2) | collective-permute-done | bytes 196640 | tf_op jit(solution)/shard_map/ppermute | solution.py:13
  65.4 1.1 collective-permute-done.3
  66.4 0.0 copy-done.2
  66.5 0.9 fusion.25
  67.4 18.2 %reduce-scatter.10.cloned.1.call-done = f32[64,256]{1,0:T(8,128)} async-done(((f32[512,256]{1,0:T(8,128)}), f32[64,256]{1,0:T(8,128)}) %reduce-scatter.10.cloned.1.call-update) | async-done | bytes 65552
  85.6 0.9 copy.21
  86.5 0.7 copy.16
  87.3 30.6 %reduce-scatter.8.cloned.1.call-done = f32[32,512]{1,0:T(8,128)} async-done(((f32[256,512]{1,0:T(8,128)}), f32[32,512]{1,0:T(8,128)}) %reduce-scatter.8.cloned.1.call-update) | async-done | bytes 65552 | tf_op jit(solution)/shard_map/reduce_scatter | solution.py:82
  117.9 41.3 %reduce-scatter.6.cloned.1.call-done = f32[64,3,512]{2,0,1:T(8,128)} async-done(((f32[512,3,512]{2,0,1:T(8,128)}), f32[64,3,512]{2,0,1:T(8,128)}) %reduce-scatter.6.cloned.1.call-update) | async-done | bytes 393232 | tf_op jit(solution)/shard_map/reduce_scatter | solution.py:80
  (1 shorter events, 0.0 us)
Async XLA Ops:
  7.2 24.3 %copy-start = (bf16[1,256,512]{2,1,0:T(8,128)(2,1)S(1)}, bf16[1,256,512]{2,1,0:T(8,128)(2,1)}, u32[]{:S(2)}) copy-start(bf16[1,256,512]{2,1,0:T(8,128)(2,1)} %param.8) | copy-start | bytes 786436
  7.2 24.5 %copy-start.1 = (bf16[192,1,512]{2,0,1:T(8,128)(2,1)S(1)}, bf16[192,1,512]{2,0,1:T(8,128)(2,1)}, u32[]{:S(2)}) copy-start(bf16[192,1,512]{2,0,1:T(8,128)(2,1)} %param.5) | copy-start | bytes 589828
  7.2 24.5 %copy-start.3 = (bf16[192,1,512]{2,0,1:T(8,128)(2,1)S(1)}, bf16[192,1,512]{2,0,1:T(8,128)(2,1)}, u32[]{:S(2)}) copy-start(bf16[192,1,512]{2,0,1:T(8,128)(2,1)} %param.9) | copy-start | bytes 589828
  7.2 78.4 %reduce-scatter.10.cloned.1.call-start = ((), (), s32[]{:S(2)}) async-start(), calls=%async_computation.5 | async-start | bytes 589824
  7.2 24.5 %collective-permute-start.1 = (bf16[192,512]{1,0:T(8,128)(2,1)}, bf16[192,512]{1,0:T(8,128)(2,1)S(1)}, u32[]{:S(2)}, u32[]{:S(2)}) collective-permute-start(bf16[192,512]{1,0:T(8,128)(2,1)} %bitcast.69), channel_id=1, source_target_pairs={{0,2},{1,3},{2,0},{3,1},{4,6},{5,7},{6,4},{7,5},{8,10},{9,11},{10,... | collective-permute-start | bytes 589832 | tf_op jit(solution)/shard_map/ppermute | solution.py:13
  10.3 21.4 %collective-permute-start = (bf16[192,512]{1,0:T(8,128)(2,1)}, bf16[192,512]{1,0:T(8,128)(2,1)S(1)}, u32[]{:S(2)}, u32[]{:S(2)}) collective-permute-start(bf16[192,512]{1,0:T(8,128)(2,1)} %bitcast.70), channel_id=1, source_target_pairs={{0,1},{1,0},{2,3},{3,2},{4,5},{5,4},{6,7},{7,6},{8,9},{9,8},{10,11... | collective-permute-start | bytes 589832 | tf_op jit(solution)/shard_map/ppermute | solution.py:13
  53.8 64.1 %reduce-scatter.8.cloned.1.call-start = ((), (), s32[]{:S(2)}) async-start(), calls=%async_computation.4 | async-start | bytes 589824 | tf_op jit(solution)/shard_map/reduce_scatter | solution.py:82
  54.9 104.2 %reduce-scatter.6.cloned.1.call-start = ((), (), s32[]{:S(2)}) async-start(), calls=%async_computation.3 | async-start | bytes 3538944 | tf_op jit(solution)/shard_map/reduce_scatter | solution.py:80
  59.1 7.4 %copy-start.2 = (bf16[1,512,256]{2,1,0:T(8,128)(2,1)S(1)}, bf16[1,512,256]{2,1,0:T(8,128)(2,1)}, u32[]{:S(2)}) copy-start(bf16[1,512,256]{2,1,0:T(8,128)(2,1)} %param.7) | copy-start | bytes 786436
  59.6 5.7 %collective-permute-start.2 = (bf16[192,512]{1,0:T(8,128)(2,1)S(1)}, bf16[192,512]{1,0:T(8,128)(2,1)S(1)}, u32[]{:S(2)}, u32[]{:S(2)}) collective-permute-start(bf16[192,512]{1,0:T(8,128)(2,1)S(1)} %get-tuple-element.20), channel_id=1, source_target_pairs={{0,1},{1,0},{2,3},{3,2},{4,5},{5,4},{6,7},{7,6},{8,9},{9,8},{10,11... | collective-permute-start | bytes 589832 | tf_op jit(solution)/shard_map/ppermute | solution.py:13
  60.8 5.7 %collective-permute-start.3 = (bf16[192,512]{1,0:T(8,128)(2,1)S(1)}, bf16[192,512]{1,0:T(8,128)(2,1)S(1)}, u32[]{:S(2)}, u32[]{:S(2)}) collective-permute-start(bf16[192,512]{1,0:T(8,128)(2,1)S(1)} %get-tuple-element.21), channel_id=1, source_target_pairs={{0,2},{1,3},{2,0},{3,1},{4,6},{5,7},{6,4},{7,5},{8,10},{9,11},{10,... | collective-permute-start | bytes 589832 | tf_op jit(solution)/shard_map/ppermute | solution.py:13
Sparse Core Ops, SparseCore 0:
  53.9 31.6 reduce-scatter.9
  88.4 29.3 reduce-scatter.7
  120.7 38.3 reduce-scatter.5
where the time goes:
time: 166 us
  waiting for transfers between devices  94.6 us (57%)
  blocking collectives  36 us (22%)
  between operations  13.9 us (8%)
  matrix products  9.9 us (6%)
  starting transfers between devices  6.78 us (4%)
  local copies, waits for them, and re-layouts  4.47 us (3%)
    reduce_scatter x1, waiting for transfers between devices, shards(): lax.psum_scatter(block_term, 'dp', scatter_dimension=0, tiled=True)  41.3 us
    reduce_scatter x1, waiting for transfers between devices, shards(): lax.psum_scatter(right_term, 'dp', scatter_dimension=0, tiled=True)  30.6 us
    psum x1, blocking collectives, shards(): lax.psum(jnp.dot(own_x, left, preferred_element_type=jnp.float32), 'width')  18.4 us
    unnamed x4, waiting for transfers between devices  18.3 us
    psum x1, blocking collectives, shards(): latent_grad = lax.psum(latent_term, 'width').astype(jnp.bfloat16)  17.6 us
    ppermute x4, starting transfers between devices, swapped(): lax.ppermute(array, axis, [(i, i ^ 1 << apart) for i in range(lax.axis_si...  6.66 us
    ppermute x4, waiting for transfers between devices, swapped(): lax.ppermute(array, axis, [(i, i ^ 1 << apart) for i in range(lax.axis_si...  4.41 us
    unnamed x12, local copies, waits for them, and re-layouts  4.38 us
  transfers between devices with their start and end apart: 7, of which 5 were waited for; matrix products, arithmetic and copies ran while one was open for 6% of the time, Pallas kernels for 0%

commit v1 on v0

--- a/solution.py
+++ b/solution.py
@@ -1,8 +1,11 @@
+import functools
 import math
 
 import jax
 import jax.numpy as jnp
 from jax import lax
+from jax.experimental import pallas as pl
+from jax.experimental.pallas import tpu as pltpu
 from jax.sharding import PartitionSpec as P
 
 root_half = 0.7071067811865476
@@ -23,7 +26,7 @@
     )
 
 
-def shards(inputs, block_weights, low_left, low_right, out_grad):
+def plain_shards(inputs, block_weights, low_left, low_right, out_grad):
     own_x = inputs[:, 0]
     weights = block_weights[0]
     left = low_left[0]
@@ -90,6 +93,380 @@
     )
 
 
+f32 = jnp.float32
+bf16 = jnp.bfloat16
+
+
+def dot_nn(a, b):
+    return jnp.dot(a, b, preferred_element_type=f32)
+
+
+def dot_nt(a, b):
+    return lax.dot_general(a, b, (((1,), (1,)), ((), ())), preferred_element_type=f32)
+
+
+def remote(src, dst, send, recv, dp, width):
+    return pltpu.make_async_remote_copy(
+        src_ref=src,
+        dst_ref=dst,
+        send_sem=send,
+        recv_sem=recv,
+        device_id={"dp": dp, "width": width},
+        device_id_type=pl.DeviceIdType.MESH,
+    )
+
+
+def step_kernel(
+    n_dp, n_width, scale,
+    x_hbm, w_hbm, left_hbm, right_hbm, g_hbm,
+    act_out, in_out, block_out, left_out, right_out,
+    x, w, left, right, g,
+    xs, lat_own, lat_got, lg_own, lg_got, hidden, x_t, h_t, lat_t,
+    back_own, back_got, pre, own_back,
+    main_away, main_own, main_core, main_send, main_lo, main_hi, main_sum,
+    low_away, low_own, low_core, low_send, low_lo, low_hi, low_sum,
+    load_sem, x_send, x_recv, lat_send, lat_recv, lg_send, lg_recv, back_send, back_recv,
+    core_send, core_recv, line_send, lo_recv, hi_recv,
+):
+    levels = n_width.bit_length() - 1
+    chips = n_dp // 2
+    dp = lax.axis_index("dp")
+    me = lax.axis_index("width")
+    chip, core = dp // 2, dp % 2
+    other_core = 1 - core
+    twin = dp + 1 - 2 * core
+
+    def mate(k):
+        at = me
+        for bit in range(levels):
+            if k >> bit & 1:
+                at = at + (1 << bit) * (1 - 2 * ((me // (1 << bit)) % 2))
+        return at
+
+    barrier = pltpu.get_barrier_semaphore()
+
+    def greet(to_dp, to_width):
+        pl.semaphore_signal(
+            barrier,
+            inc=1,
+            device_id={"dp": to_dp, "width": to_width},
+            device_id_type=pl.DeviceIdType.MESH,
+        )
+
+    for k in range(1, n_width):
+        greet(dp, mate(k))
+    greet(twin, me)
+
+    @pl.when(chip > 0)
+    def _():
+        greet(dp - 2, me)
+
+    @pl.when(chip < chips - 1)
+    def _():
+        greet(dp + 2, me)
+
+    loads = [
+        pltpu.make_async_copy(src, dst, load_sem.at[i])
+        for i, (src, dst) in enumerate(
+            ((x_hbm, x), (left_hbm, left), (w_hbm, w), (right_hbm, right), (g_hbm, g))
+        )
+    ]
+    for load in loads:
+        load.start()
+
+    ends = jnp.where(chip == 0, 1, 0) + jnp.where(chip == chips - 1, 1, 0)
+    pl.semaphore_wait(barrier, n_width + 2 - ends)
+
+    loads[0].wait()
+    x_copies = [
+        remote(x, xs.at[bit], x_send.at[bit], x_recv.at[bit], dp, mate(1 << bit))
+        for bit in range(levels)
+    ]
+    loads[1].wait()
+    lat_mine = dot_nn(x[...], left[...])
+    lat_own[...] = lat_mine.astype(bf16)
+    lat_copies = [
+        remote(lat_own, lat_got.at[k - 1], lat_send.at[k - 1], lat_recv.at[k - 1], dp, mate(k))
+        for k in range(1, n_width)
+    ]
+    for copy in lat_copies:
+        copy.start()
+    for copy in x_copies:
+        copy.start()
+    loads[2].wait()
+    pre[...] = dot_nt(x[...], w[0])
+    x_t[...] = x[...].astype(f32).T.astype(bf16).reshape(x_t.shape)
+    loads[3].wait()
+    loads[4].wait()
+    for copy in lat_copies:
+        copy.wait_recv()
+    lat_sum = lat_mine
+    for k in range(n_width - 1):
+        lat_sum = lat_sum + lat_got[k].astype(f32)
+    latent = lat_sum.astype(bf16)
+    lat_t[...] = lat_sum.T.astype(bf16).reshape(lat_t.shape)
+    pre[...] += dot_nn(latent, right[...])
+    for bit in range(levels):
+        x_copies[bit].wait_recv()
+        pre[...] += dot_nt(xs[bit], w[bit + 1])
+
+    v = pre[...]
+    half = 0.5 * (1.0 + lax.erf(v * root_half))
+    act_out[...] = (v * half).astype(bf16)
+    slope = half + v * jnp.exp(-0.5 * v * v) * inv_root_two_pi
+    hid = g[...].astype(f32) * slope
+    hidden[...] = hid.astype(bf16)
+    h = hidden[...]
+    lg_mine = dot_nt(h, right[...])
+    lg_own[...] = lg_mine.astype(bf16)
+    lg_copies = [
+        remote(lg_own, lg_got.at[k - 1], lg_send.at[k - 1], lg_recv.at[k - 1], dp, mate(k))
+        for k in range(1, n_width)
+    ]
+    for copy in lg_copies:
+        copy.start()
+    h_t[...] = h.astype(f32).T.astype(bf16).reshape(h_t.shape)
+
+    ob, rb = h_t.shape[2], lat_t.shape[2]
+    rows = h_t.shape[3]
+
+    def main_terms(which, out_ref):
+        lhs = h_t[:, which].reshape(chips * ob, rows)
+        for level in range(levels + 1):
+            rhs = x[...] if level == 0 else xs[level - 1]
+            term = dot_nn(lhs, rhs).astype(out_ref.dtype)
+            out_ref[:, level * ob : (level + 1) * ob, :] = term.reshape(chips, ob, term.shape[1])
+        lhs = lat_t[:, which].reshape(chips * rb, rows)
+        term = dot_nn(lhs, hidden[...]).astype(out_ref.dtype)
+        out_ref[:, (levels + 1) * ob :, :] = term.reshape(chips, rb, term.shape[1])
+
+    far_first = []
+    for k in range((chips + 1) // 2):
+        far_first += [chips - 1 - k, k] if chips - 1 - k != k else [k]
+    away = (main_away, low_away)
+    own = (main_own, low_own)
+    got_core = (main_core, low_core)
+    sends = (main_send, low_send)
+    got_lo = (main_lo, low_lo)
+    got_hi = (main_hi, low_hi)
+    sums = (main_sum, low_sum)
+
+    def core_copy(s, c):
+        return remote(
+            away[s].at[c], got_core[s].at[c], core_send.at[s, c], core_recv.at[s, c], twin, me
+        )
+
+    def up_copy(s, c, to):
+        return remote(
+            sends[s].at[c], got_lo[s].at[c], line_send.at[s, c], lo_recv.at[s, c], to, me
+        )
+
+    def down_copy(s, c, to):
+        return remote(
+            sends[s].at[c], got_hi[s].at[c], line_send.at[s, c], hi_recv.at[s, c], to, me
+        )
+
+    def pair_sum(s, c):
+        core_copy(s, c).wait_recv()
+        return own[s][c] + got_core[s][c].astype(f32)
+
+    def first_hops(s):
+        for k in range(chips - 1):
+            c = chips - 1 - k
+
+            @pl.when(chip == 0)
+            def _():
+                sends[s][c] = pair_sum(s, c).astype(bf16)
+                up_copy(s, c, dp + 2).start()
+
+            @pl.when(chip == chips - 1)
+            def _():
+                sends[s][k] = pair_sum(s, k).astype(bf16)
+                down_copy(s, k, dp - 2).start()
+
+    def later_hops(s, k):
+        c = chips - 1 - k
+
+        @pl.when((chip > 0) & (chip < c))
+        def _():
+            total = pair_sum(s, c)
+            up_copy(s, c, dp + 2).wait_recv()
+            sends[s][c] = (total + got_lo[s][c].astype(f32)).astype(bf16)
+            up_copy(s, c, dp + 2).start()
+
+        @pl.when((chip < chips - 1) & (chip > k))
+        def _():
+            total = pair_sum(s, k)
+            down_copy(s, k, dp - 2).wait_recv()
+            sends[s][k] = (total + got_hi[s][k].astype(f32)).astype(bf16)
+            down_copy(s, k, dp - 2).start()
+
+    def finish(s):
+        sums[s][...] = pair_sum(s, chip)
+
+        @pl.when(chip > 0)
+        def _():
+            up_copy(s, chip, dp - 2).wait_recv()
+            sums[s][...] += got_lo[s][chip].astype(f32)
+
+        @pl.when(chip < chips - 1)
+        def _():
+            down_copy(s, chip, dp + 2).wait_recv()
+            sums[s][...] += got_hi[s][chip].astype(f32)
+
+    main_terms(other_core, main_away)
+    for c in far_first:
+        core_copy(0, c).start()
+    main_terms(core, main_own)
+    first_hops(0)
+
+    back_copies = []
+    for bit in range(levels):
+        back_own[bit] = dot_nn(hidden[...], w[bit + 1]).astype(bf16)
+        copy = remote(
+            back_own.at[bit], back_got.at[bit], back_send.at[bit], back_recv.at[bit],
+            dp, mate(1 << bit),
+        )
+        copy.start()
+        back_copies.append(copy)
+
+    for copy in lg_copies:
+        copy.wait_recv()
+    for k in range(n_width - 1):
+        lg_mine = lg_mine + lg_got[k].astype(f32)
+    latent_grad = lg_mine.astype(bf16)
+
+    def low_terms(which, out_ref):
+        lhs = x_t[:, which].reshape(chips * x_t.shape[2], rows)
+        term = dot_nn(lhs, latent_grad).astype(out_ref.dtype)
+        out_ref[...] = term.reshape(out_ref.shape)
+
+    low_terms(other_core, low_away)
+    for c in far_first:
+        core_copy(1, c).start()
+    low_terms(core, low_own)
+    first_hops(1)
+    own_back[...] = dot_nn(hidden[...], w[0]) + dot_nt(latent_grad, left[...])
+    for k in range(chips - 2):
+        later_hops(0, k)
+    for k in range(chips - 2):
+        later_hops(1, k)
+    total = own_back[...]
+    for bit in range(levels):
+        back_copies[bit].wait_recv()
+        total = total + back_got[bit].astype(f32)
+    in_out[...] = total.astype(bf16)
+    finish(0)
+    for level in range(levels + 1):
+        block_out[level] = main_sum[level * ob : (level + 1) * ob, :] * scale
+    right_out[...] = main_sum[(levels + 1) * ob :, :] * scale
+    finish(1)
+    left_out[...] = low_sum[...] * scale
+
+    for copy in x_copies + lat_copies + lg_copies + back_copies:
+        copy.wait_send()
+    for s in range(2):
+        for c in range(chips):
+            core_copy(s, c).wait_send()
+
+            @pl.when(chip != c)
+            def _():
+                up_copy(s, c, twin).wait_send()
+
+
+def shards(inputs, block_weights, low_left, low_right, out_grad):
+    n_dp, n_width = lax.axis_size("dp"), lax.axis_size("width")
+    levels = n_width.bit_length() - 1
+    rows, _, width_in = inputs.shape
+    width_out = block_weights.shape[1]
+    rank = low_left.shape[2]
+    ob, ib, rb = width_out // n_dp, width_in // n_dp, rank // n_dp
+    fits = n_dp % 2 == 0 and rows % 16 == 0 and width_in == width_out
+    if not fits or ob % 16 or ib % 16 or rb % 16 or width_in % 128 or rank % 128:
+        return plain_shards(inputs, block_weights, low_left, low_right, out_grad)
+    chips = n_dp // 2
+    scale = 1.0 / math.sqrt(rows * n_dp)
+    main = (levels + 1) * ob + rb
+    vm, dma = pltpu.VMEM, pltpu.SemaphoreType.DMA
+
+    def line_scratch(r, c):
+        return [
+            vm((chips, r, c), bf16),
+            vm((chips, r, c), f32),
+            vm((chips, r, c), bf16),
+            vm((chips, r, c), bf16),
+            vm((chips, r, c), bf16),
+            vm((chips, r, c), bf16),
+            vm((r, c), f32),
+        ]
+
+    outs = pl.pallas_call(
+        functools.partial(step_kernel, n_dp, n_width, scale),
+        out_shape=(
+            jax.ShapeDtypeStruct((rows, width_out), bf16),
+            jax.ShapeDtypeStruct((rows, width_in), bf16),
+            jax.ShapeDtypeStruct((levels + 1, ob, width_in), f32),
+            jax.ShapeDtypeStruct((ib, rank), f32),
+            jax.ShapeDtypeStruct((rb, width_out), f32),
+        ),
+        in_specs=[pl.BlockSpec(memory_space=pltpu.HBM)] * 5,
+        out_specs=(pl.BlockSpec(memory_space=pltpu.VMEM),) * 5,
+        scratch_shapes=[
+            vm((rows, width_in), bf16),
+            vm((levels + 1, width_out, width_in), bf16),
+            vm((width_in, rank), bf16),
+            vm((rank, width_out), bf16),
+            vm((rows, width_out), bf16),
+            vm((levels, rows, width_in), bf16),
+            vm((rows, rank), bf16),
+            vm((n_width - 1, rows, rank), bf16),
+            vm((rows, rank), bf16),
+            vm((n_width - 1, rows, rank), bf16),
+            vm((rows, width_out), bf16),
+            vm((chips, 2, ib, rows), bf16),
+            vm((chips, 2, ob, rows), bf16),
+            vm((chips, 2, rb, rows), bf16),
+            vm((levels, rows, width_in), bf16),
+            vm((levels, rows, width_in), bf16),
+            vm((rows, width_out), f32),
+            vm((rows, width_in), f32),
+            *line_scratch(main, width_in),
+            *line_scratch(ib, rank),
+            dma((5,)),
+            dma((levels,)),
+            dma((levels,)),
+            dma((n_width - 1,)),
+            dma((n_width - 1,)),
+            dma((n_width - 1,)),
+            dma((n_width - 1,)),
+            dma((levels,)),
+            dma((levels,)),
+            dma((2, chips)),
+            dma((2, chips)),
+            dma((2, chips)),
+            dma((2, chips)),
+            dma((2, chips)),
+        ],
+        compiler_params=pltpu.CompilerParams(
+            collective_id=0, has_side_effects=True, vmem_limit_bytes=40 * 1024 * 1024
+        ),
+    )(
+        inputs[:, 0],
+        block_weights[0].transpose(1, 0, 2),
+        low_left[0],
+        low_right[0],
+        out_grad[:, 0],
+    )
+    act, in_grad, block, left, right = outs
+    return (
+        act[:, None],
+        in_grad[:, None],
+        block.transpose(1, 0, 2)[None],
+        left[None],
+        right[None],
+    )
+
+
 def solution(mesh):
     placed = (
         P("dp", "width", None),

time: 166 us -> 59.2 us (0.36)
  waiting for transfers between devices: 94.6 us -> 0 us
  Pallas kernels: 0 us -> 49.8 us
  blocking collectives: 36 us -> 0 us
  between operations: 13.9 us -> 0.66 us
  matrix products: 9.9 us -> 0 us
  starting transfers between devices: 6.78 us -> 0 us
  local copies, waits for them, and re-layouts: 4.47 us -> 8.51 us
    reduce_scatter x2 -> x0, waiting for transfers between devices: 71.9 us -> none  [the longest x1 41.3 us: shards(): lax.psum_scatter(block_term, 'dp', scatter_dimension=0, tiled=True)]
    pallas_call x0 -> x1, Pallas kernels: none -> 49.8 us  [shards(): pl.pallas_call(functools.partial(step_kernel, n_dp, n_width, scale), out_...]
    psum x2 -> x0, blocking collectives: 36 us -> none  [the longest x1 18.4 us: shards(): lax.psum(jnp.dot(own_x, left, preferred_element_type=jnp.float32), 'width')]
    unnamed x4 -> x0, waiting for transfers between devices: 18.3 us -> none
    dot_general x10 -> x0, matrix products: 9.9 us -> none  [the longest x1 2.92 us: shards(): lax.dot_general(all_x, weights, (((1, 2), (1, 2)), ((), ())), preferred_e...]
    ppermute x4 -> x0, starting transfers between devices: 6.66 us -> none  [swapped(): lax.ppermute(array, axis, [(i, i ^ 1 << apart) for i in range(lax.axis_si...]
    ppermute x4 -> x0, waiting for transfers between devices: 4.41 us -> none  [swapped(): lax.ppermute(array, axis, [(i, i ^ 1 << apart) for i in range(lax.axis_si...]
    unnamed x12 -> x15, local copies, waits for them, and re-layouts: 4.38 us -> 8.51 us
  transfers between devices with their start and end apart: 7 -> 0, of which waited for: 5 -> 0; matrix products, arithmetic and copies ran while one was open for 6% -> 0% of each run, Pallas kernels for 0% -> 0%
where the time goes in v1:
time: 59.2 us; the launch traced here: 59 us
  Pallas kernels  49.8 us (84%)
  local copies, waits for them, and re-layouts  8.51 us (14%)
  between operations  0.66 us (1%)
    pallas_call x1, Pallas kernels, shards(): pl.pallas_call(functools.partial(step_kernel, n_dp, n_width, scale), out_...  49.8 us
    unnamed x15, local copies, waits for them, and re-layouts  8.51 us

profile of v1, /device:TPU:0, one launch (start us, length us, event | category | flops | bytes accessed | tf_op | source)
XLA Modules:
  0.0 59.0 jit_solution(13534342581594964769)
XLA Ops:
  0.6 0.0 copy-start
  0.6 1.4 %copy-done = bf16[1,512,3,512]{3,1,2,0:T(8,128)(2,1)S(1)} copy-done((bf16[1,512,3,512]{3,1,2,0:T(8,128)(2,1)S(1)}, bf16[1,512,3,512]{3,1,2,0:T(8,128)(2,1)}, u32[]{:S(2)}) %copy-start) | copy-done | bytes 1572888
  2.0 0.0 copy-start.1
  2.0 0.9 %copy-done.1 = bf16[1,512,256]{2,1,0:T(8,128)(2,1)S(1)} copy-done((bf16[1,512,256]{2,1,0:T(8,128)(2,1)S(1)}, bf16[1,512,256]{2,1,0:T(8,128)(2,1)}, u32[]{:S(2)}) %copy-start.1) | copy-done | bytes 262168
  3.0 0.0 copy-start.2
  3.0 0.9 %copy-done.2 = bf16[1,256,512]{2,1,0:T(8,128)(2,1)S(1)} copy-done((bf16[1,256,512]{2,1,0:T(8,128)(2,1)S(1)}, bf16[1,256,512]{2,1,0:T(8,128)(2,1)}, u32[]{:S(2)}) %copy-start.2) | copy-done | bytes 262168
  3.9 0.0 copy-start.3
  3.9 0.9 %copy-done.3 = bf16[192,1,512]{2,0,1:T(8,128)(2,1)S(1)} copy-done((bf16[192,1,512]{2,0,1:T(8,128)(2,1)S(1)}, bf16[192,1,512]{2,0,1:T(8,128)(2,1)}, u32[]{:S(2)}) %copy-start.3) | copy-done | bytes 196632
  4.9 0.0 copy-start.4
  4.9 0.9 %copy-done.4 = bf16[192,1,512]{2,0,1:T(8,128)(2,1)S(1)} copy-done((bf16[192,1,512]{2,0,1:T(8,128)(2,1)S(1)}, bf16[192,1,512]{2,0,1:T(8,128)(2,1)}, u32[]{:S(2)}) %copy-start.4) | copy-done | bytes 196632
  5.8 49.8 %shard_map.92 = (bf16[192,512]{1,0:T(8,128)(2,1)S(1)}, bf16[192,512]{1,0:T(8,128)(2,1)S(1)}, f32[3,64,512]{2,1,0:T(8,128)S(1)}, f32[64,256]{1,0:T(8,128)S(1)}, f32[32,512]{1,0:T(8,128)S(1)}) custom-call(bf16[192,512]{1,0:T(8,128)(2,1)S(1)} %bitcast.18, bf16[3,512,512]{2,1,0:T(8,128)(2,1)S(1)} %bitcast.14, bf16[512,256]{1,0:T(8,128)(2,1)S(1)} %bitcast.16, ...), custom_call_target="tpu_custom_call" | custom-call | tf_op jit(solution)/shard_map/pallas_call | solution.py:403
  55.6 0.7 %copy.15 = bf16[192,1,512]{2,0,1:T(8,128)(2,1)} copy(bf16[192,1,512]{2,0,1:T(8,128)(2,1)S(1)} %bitcast.21) | data formatting | bytes 393216
  56.3 0.7 %copy.16 = bf16[192,1,512]{2,0,1:T(8,128)(2,1)} copy(bf16[192,1,512]{2,0,1:T(8,128)(2,1)S(1)} %bitcast.20) | data formatting | bytes 393216
  57.0 0.7 %copy.17 = f32[1,64,3,512]{3,1,2,0:T(8,128)} copy(f32[1,64,3,512]{3,1,2,0:T(8,128)S(1)} %bitcast.15) | data formatting | bytes 786432
  57.7 0.6 %copy.18 = f32[1,64,256]{2,1,0:T(8,128)} copy(f32[1,64,256]{2,1,0:T(8,128)S(1)} %bitcast.23) | data formatting | bytes 131072
  58.4 0.6 %copy.19 = f32[1,32,512]{2,1,0:T(8,128)} copy(f32[1,32,512]{2,1,0:T(8,128)S(1)} %bitcast.22) | data formatting | bytes 131072
Async XLA Ops:
  0.6 1.4 %copy-start = (bf16[1,512,3,512]{3,1,2,0:T(8,128)(2,1)S(1)}, bf16[1,512,3,512]{3,1,2,0:T(8,128)(2,1)}, u32[]{:S(2)}) copy-start(bf16[1,512,3,512]{3,1,2,0:T(8,128)(2,1)} %param.6) | copy-start | bytes 4718596
  2.0 0.9 %copy-start.1 = (bf16[1,512,256]{2,1,0:T(8,128)(2,1)S(1)}, bf16[1,512,256]{2,1,0:T(8,128)(2,1)}, u32[]{:S(2)}) copy-start(bf16[1,512,256]{2,1,0:T(8,128)(2,1)} %param.7) | copy-start | bytes 786436
  3.0 0.9 %copy-start.2 = (bf16[1,256,512]{2,1,0:T(8,128)(2,1)S(1)}, bf16[1,256,512]{2,1,0:T(8,128)(2,1)}, u32[]{:S(2)}) copy-start(bf16[1,256,512]{2,1,0:T(8,128)(2,1)} %param.8) | copy-start | bytes 786436
  3.9 0.9 %copy-start.3 = (bf16[192,1,512]{2,0,1:T(8,128)(2,1)S(1)}, bf16[192,1,512]{2,0,1:T(8,128)(2,1)}, u32[]{:S(2)}) copy-start(bf16[192,1,512]{2,0,1:T(8,128)(2,1)} %param.5) | copy-start | bytes 589828
  4.9 0.9 %copy-start.4 = (bf16[192,1,512]{2,0,1:T(8,128)(2,1)S(1)}, bf16[192,1,512]{2,0,1:T(8,128)(2,1)}, u32[]{:S(2)}) copy-start(bf16[192,1,512]{2,0,1:T(8,128)(2,1)} %param.9) | copy-start | bytes 589828

commit v2 on v1

--- a/solution.py
+++ b/solution.py
@@ -123,8 +123,8 @@
     x, w, left, right, g,
     xs, lat_own, lat_got, lg_own, lg_got, hidden, x_t, h_t, lat_t,
     back_own, back_got, pre, own_back,
-    main_away, main_own, main_core, main_send, main_lo, main_hi, main_sum,
-    low_away, low_own, low_core, low_send, low_lo, low_hi, low_sum,
+    main_away, main_own, main_core, main_send, main_lo, main_hi,
+    low_away, low_own, low_core, low_send, low_lo, low_hi,
     load_sem, x_send, x_recv, lat_send, lat_recv, lg_send, lg_recv, back_send, back_recv,
     core_send, core_recv, line_send, lo_recv, hi_recv,
 ):
@@ -230,96 +230,85 @@
     ob, rb = h_t.shape[2], lat_t.shape[2]
     rows = h_t.shape[3]
 
-    def main_terms(which, out_ref):
+    last = levels + 1
+
+    def main_terms(which, out_ref, level):
         lhs = h_t[:, which].reshape(chips * ob, rows)
-        for level in range(levels + 1):
-            rhs = x[...] if level == 0 else xs[level - 1]
-            term = dot_nn(lhs, rhs).astype(out_ref.dtype)
-            out_ref[:, level * ob : (level + 1) * ob, :] = term.reshape(chips, ob, term.shape[1])
-        lhs = lat_t[:, which].reshape(chips * rb, rows)
-        term = dot_nn(lhs, hidden[...]).astype(out_ref.dtype)
-        out_ref[:, (levels + 1) * ob :, :] = term.reshape(chips, rb, term.shape[1])
+        rhs = x[...] if level == 0 else xs[level - 1]
+        term = dot_nn(lhs, rhs).astype(out_ref.dtype)
+        out_ref[:, level * ob : (level + 1) * ob, :] = term.reshape(chips, ob, term.shape[1])
+        if level == levels:
+            lhs = lat_t[:, which].reshape(chips * rb, rows)
+            term = dot_nn(lhs, hidden[...]).astype(out_ref.dtype)
+            out_ref[:, last * ob :, :] = term.reshape(chips, rb, term.shape[1])
 
     far_first = []
     for k in range((chips + 1) // 2):
         far_first += [chips - 1 - k, k] if chips - 1 - k != k else [k]
-    away = (main_away, low_away)
-    own = (main_own, low_own)
-    got_core = (main_core, low_core)
-    sends = (main_send, low_send)
-    got_lo = (main_lo, low_lo)
-    got_hi = (main_hi, low_hi)
-    sums = (main_sum, low_sum)
+
+    def part(main_ref, low_ref, s, c):
+        if s == last:
+            return low_ref.at[c]
+        top = (s + 1) * ob + (rb if s == levels else 0)
+        return main_ref.at[c, s * ob : top]
 
     def core_copy(s, c):
         return remote(
-            away[s].at[c], got_core[s].at[c], core_send.at[s, c], core_recv.at[s, c], twin, me
+            part(main_away, low_away, s, c), part(main_core, low_core, s, c),
+            core_send.at[s, c], core_recv.at[s, c], twin, me,
         )
 
     def up_copy(s, c, to):
         return remote(
-            sends[s].at[c], got_lo[s].at[c], line_send.at[s, c], lo_recv.at[s, c], to, me
+            part(main_send, low_send, s, c), part(main_lo, low_lo, s, c),
+            line_send.at[s, c], lo_recv.at[s, c], to, me,
         )
 
     def down_copy(s, c, to):
         return remote(
-            sends[s].at[c], got_hi[s].at[c], line_send.at[s, c], hi_recv.at[s, c], to, me
+            part(main_send, low_send, s, c), part(main_hi, low_hi, s, c),
+            line_send.at[s, c], hi_recv.at[s, c], to, me,
         )
 
     def pair_sum(s, c):
         core_copy(s, c).wait_recv()
-        return own[s][c] + got_core[s][c].astype(f32)
-
-    def first_hops(s):
-        for k in range(chips - 1):
-            c = chips - 1 - k
-
-            @pl.when(chip == 0)
-            def _():
-                sends[s][c] = pair_sum(s, c).astype(bf16)
-                up_copy(s, c, dp + 2).start()
-
-            @pl.when(chip == chips - 1)
-            def _():
-                sends[s][k] = pair_sum(s, k).astype(bf16)
-                down_copy(s, k, dp - 2).start()
-
-    def later_hops(s, k):
-        c = chips - 1 - k
-
-        @pl.when((chip > 0) & (chip < c))
-        def _():
-            total = pair_sum(s, c)
+        return part(main_own, low_own, s, c)[...] + part(main_core, low_core, s, c)[...].astype(f32)
+
+    messages = [(k, s) for k in range(chips - 2) for s in range(last)]
+    early = len(messages)
+    messages += [(k, last) for k in range(chips - 2)]
+    messages += [(chips - 2, s) for s in range(last + 1)]
+
+    def hop(z, up, k, s):
+        c = chips - 1 - k if up else k
+        total = pair_sum(s, c)
+        if up and z > 0:
             up_copy(s, c, dp + 2).wait_recv()
-            sends[s][c] = (total + got_lo[s][c].astype(f32)).astype(bf16)
+            total = total + part(main_lo, low_lo, s, c)[...].astype(f32)
+        if not up and z < chips - 1:
+            down_copy(s, c, dp - 2).wait_recv()
+            total = total + part(main_hi, low_hi, s, c)[...].astype(f32)
+        part(main_send, low_send, s, c)[...] = total.astype(bf16)
+        if up:
             up_copy(s, c, dp + 2).start()
-
-        @pl.when((chip < chips - 1) & (chip > k))
-        def _():
-            total = pair_sum(s, k)
-            down_copy(s, k, dp - 2).wait_recv()
-            sends[s][k] = (total + got_hi[s][k].astype(f32)).astype(bf16)
-            down_copy(s, k, dp - 2).start()
-
-    def finish(s):
-        sums[s][...] = pair_sum(s, chip)
-
-        @pl.when(chip > 0)
-        def _():
-            up_copy(s, chip, dp - 2).wait_recv()
-            sums[s][...] += got_lo[s][chip].astype(f32)
-
-        @pl.when(chip < chips - 1)
-        def _():
-            down_copy(s, chip, dp + 2).wait_recv()
-            sums[s][...] += got_hi[s][chip].astype(f32)
-
-    main_terms(other_core, main_away)
-    for c in far_first:
-        core_copy(0, c).start()
-    main_terms(core, main_own)
-    first_hops(0)
-
+        else:
+            down_copy(s, c, dp - 2).start()
+
+    def hops(z):
+        found = []
+        for index, (k, s) in enumerate(messages):
+            for up in (True, False):
+                depth = z if up else chips - 1 - z
+                if depth < chips - 1 and k < chips - 1 - depth:
+                    found.append((2 * depth + index, depth, up, k, s))
+        return [event[2:] for event in sorted(found)]
+
+    for level in range(last):
+        main_terms(other_core, main_away, level)
+        for c in far_first:
+            core_copy(level, c).start()
+    for level in range(last):
+        main_terms(core, main_own, level)
     back_copies = []
     for bit in range(levels):
         back_own[bit] = dot_nn(hidden[...], w[bit + 1]).astype(bf16)
@@ -330,6 +319,13 @@
         copy.start()
         back_copies.append(copy)
 
+    for z in sorted({0, chips - 1}):
+
+        @pl.when(chip == z)
+        def _():
+            for event in hops(z)[:early]:
+                hop(z, *event)
+
     for copy in lg_copies:
         copy.wait_recv()
     for k in range(n_width - 1):
@@ -343,29 +339,45 @@
 
     low_terms(other_core, low_away)
     for c in far_first:
-        core_copy(1, c).start()
+        core_copy(last, c).start()
     low_terms(core, low_own)
-    first_hops(1)
     own_back[...] = dot_nn(hidden[...], w[0]) + dot_nt(latent_grad, left[...])
-    for k in range(chips - 2):
-        later_hops(0, k)
-    for k in range(chips - 2):
-        later_hops(1, k)
+    for z in range(chips):
+
+        @pl.when(chip == z)
+        def _():
+            events = hops(z)
+            for event in events[early:] if z in (0, chips - 1) else events:
+                hop(z, *event)
+
     total = own_back[...]
     for bit in range(levels):
         back_copies[bit].wait_recv()
         total = total + back_got[bit].astype(f32)
     in_out[...] = total.astype(bf16)
-    finish(0)
-    for level in range(levels + 1):
-        block_out[level] = main_sum[level * ob : (level + 1) * ob, :] * scale
-    right_out[...] = main_sum[(levels + 1) * ob :, :] * scale
-    finish(1)
-    left_out[...] = low_sum[...] * scale
+
+    for z in range(chips):
+
+        @pl.when(chip == z)
+        def _():
+            for s in range(last + 1):
+                total = pair_sum(s, z)
+                if z > 0:
+                    up_copy(s, z, dp - 2).wait_recv()
+                    total = total + part(main_lo, low_lo, s, z)[...].astype(f32)
+                if z < chips - 1:
+                    down_copy(s, z, dp + 2).wait_recv()
+                    total = total + part(main_hi, low_hi, s, z)[...].astype(f32)
+                if s == last:
+                    left_out[...] = total * scale
+                else:
+                    block_out[s] = total[:ob] * scale
+                if s == levels:
+                    right_out[...] = total[ob:] * scale
 
     for copy in x_copies + lat_copies + lg_copies + back_copies:
         copy.wait_send()
-    for s in range(2):
+    for s in range(last + 1):
         for c in range(chips):
             core_copy(s, c).wait_send()
 
@@ -397,7 +409,6 @@
             vm((chips, r, c), bf16),
             vm((chips, r, c), bf16),
             vm((chips, r, c), bf16),
-            vm((r, c), f32),
         ]
 
     outs = pl.pallas_call(
@@ -441,14 +452,14 @@
             dma((n_width - 1,)),
             dma((levels,)),
             dma((levels,)),
-            dma((2, chips)),
-            dma((2, chips)),
-            dma((2, chips)),
-            dma((2, chips)),
-            dma((2, chips)),
+            dma((levels + 2, chips)),
+            dma((levels + 2, chips)),
+            dma((levels + 2, chips)),
+            dma((levels + 2, chips)),
+            dma((levels + 2, chips)),
         ],
         compiler_params=pltpu.CompilerParams(
-            collective_id=0, has_side_effects=True, vmem_limit_bytes=40 * 1024 * 1024
+            collective_id=0, has_side_effects=True
         ),
     )(
         inputs[:, 0],

time: 59.2 us -> 47.4 us (0.80)
  Pallas kernels: 49.8 us -> 40.2 us
  local copies, waits for them, and re-layouts: 8.51 us -> 6.3 us
    pallas_call x1, Pallas kernels: 49.8 us -> 40.2 us  [shards(): pl.pallas_call(functools.partial(step_kernel, n_dp, n_width, scale), out_...]
    unnamed x15 -> x9, local copies, waits for them, and re-layouts: 8.51 us -> 6.3 us
where the time goes in v2:
time: 47.4 us; the launch traced here: 47.2 us
  Pallas kernels  40.2 us (85%)
  local copies, waits for them, and re-layouts  6.3 us (13%)
  between operations  0.66 us (1%)
    pallas_call x1, Pallas kernels, shards(): pl.pallas_call(functools.partial(step_kernel, n_dp, n_width, scale), out_...  40.2 us
    unnamed x9, local copies, waits for them, and re-layouts  6.3 us

profile of v2, /device:TPU:0, one launch (start us, length us, event | category | flops | bytes accessed | tf_op | source)
XLA Modules:
  0.0 47.2 jit_solution(16913293632848247608)
XLA Ops:
  0.6 40.2 %shard_map.92 = (bf16[192,512]{1,0:T(8,128)(2,1)}, bf16[192,512]{1,0:T(8,128)(2,1)}, f32[3,64,512]{2,1,0:T(8,128)}, f32[64,256]{1,0:T(8,128)}, f32[32,512]{1,0:T(8,128)}) custom-call(bf16[192,512]{1,0:T(8,128)(2,1)} %bitcast.18, bf16[3,512,512]{2,1,0:T(8,128)(2,1)} %bitcast.14, bf16[512,256]{1,0:T(8,128)(2,1)} %bitcast.16, bf16[256,512]{1,0:T(8,128)(2,1)} %bitcast.17, ...), custom_call_target="tpu_custom_call" | custom-call | tf_op jit(solution)/shard_map/pallas_call | solution.py:414
  40.8 0.0 copy-start.1
  40.9 0.0 copy-start
  40.9 1.7 %copy.15 = bf16[192,1,512]{2,0,1:T(8,128)(2,1)} copy(bf16[192,1,512]{2,0,1:T(8,128)(2,1)} %bitcast.21) | data formatting | bytes 393216
  42.5 1.6 %copy.16 = bf16[192,1,512]{2,0,1:T(8,128)(2,1)} copy(bf16[192,1,512]{2,0,1:T(8,128)(2,1)} %bitcast.20) | data formatting | bytes 393216
  44.1 1.8 %copy.17 = f32[1,64,3,512]{3,1,2,0:T(8,128)} copy(f32[1,64,3,512]{3,1,2,0:T(8,128)} %bitcast.15) | data formatting | bytes 786432
  45.9 0.0 copy-done.1
  45.9 0.6 %copy.18 = f32[1,64,256]{2,1,0:T(8,128)} copy(f32[1,64,256]{2,1,0:T(8,128)S(1)} %bitcast.23) | data formatting | bytes 131072
  46.5 0.0 copy-done
  46.5 0.6 %copy.19 = f32[1,32,512]{2,1,0:T(8,128)} copy(f32[1,32,512]{2,1,0:T(8,128)S(1)} %bitcast.22) | data formatting | bytes 131072
Async XLA Ops:
  40.8 5.1 %copy-start.1 = (f32[64,256]{1,0:T(8,128)S(1)}, f32[64,256]{1,0:T(8,128)}, u32[]{:S(2)}) copy-start(f32[64,256]{1,0:T(8,128)} %get-tuple-element.13) | copy-start | bytes 196612
  40.9 5.7 %copy-start = (f32[32,512]{1,0:T(8,128)S(1)}, f32[32,512]{1,0:T(8,128)}, u32[]{:S(2)}) copy-start(f32[32,512]{1,0:T(8,128)} %get-tuple-element.14) | copy-start | bytes 196612

commit v3 on v2

--- a/solution.py
+++ b/solution.py
@@ -384,6 +384,14 @@
             @pl.when(chip != c)
             def _():
                 up_copy(s, c, twin).wait_send()
+
+
+def hand_over(*refs):
+    copies = [pltpu.make_async_copy(refs[i], refs[5 + i], refs[10].at[i]) for i in range(5)]
+    for copy in copies:
+        copy.start()
+    for copy in copies:
+        copy.wait()
 
 
 def shards(inputs, block_weights, low_left, low_right, out_grad):
@@ -459,16 +467,28 @@
             dma((levels + 2, chips)),
         ],
         compiler_params=pltpu.CompilerParams(
-            collective_id=0, has_side_effects=True
+            collective_id=0, has_side_effects=True, vmem_limit_bytes=40 * 1024 * 1024
         ),
     )(
-        inputs[:, 0],
-        block_weights[0].transpose(1, 0, 2),
-        low_left[0],
-        low_right[0],
-        out_grad[:, 0],
-    )
-    act, in_grad, block, left, right = outs
+        *(
+            pltpu.with_memory_space_constraint(array, pltpu.HBM)
+            for array in (
+                inputs[:, 0],
+                block_weights[0].transpose(1, 0, 2),
+                low_left[0],
+                low_right[0],
+                out_grad[:, 0],
+            )
+        )
+    )
+    act, in_grad, block, left, right = pl.pallas_call(
+        hand_over,
+        out_shape=tuple(jax.ShapeDtypeStruct(out.shape, out.dtype) for out in outs),
+        in_specs=[pl.BlockSpec(memory_space=pltpu.VMEM)] * 5,
+        out_specs=(pl.BlockSpec(memory_space=pl.ANY),) * 5,
+        scratch_shapes=[dma((5,))],
+        compiler_params=pltpu.CompilerParams(vmem_limit_bytes=4 * 1024 * 1024),
+    )(*outs)
     return (
         act[:, None],
         in_grad[:, None],

time: 47.4 us -> 41 us (0.86)
  local copies, waits for them, and re-layouts: 6.3 us -> 0 us
    unnamed x9 -> x0, local copies, waits for them, and re-layouts: 6.3 us -> none
    pallas_call x0 -> x1, Pallas kernels: none -> 0.96 us  [shards(): pl.pallas_call(hand_over, out_shape=tuple((jax.ShapeDtypeStruct(out.shape...]
    pallas_call x1, Pallas kernels: 40.2 us -> 39.3 us  [shards(): pl.pallas_call(functools.partial(step_kernel, n_dp, n_width, scale), out_...]
where the time goes in v3:
time: 41 us; the launch traced here: 40.9 us
  Pallas kernels  40.2 us (98%)
  between operations  0.64 us (2%)
    pallas_call x1, Pallas kernels, shards(): pl.pallas_call(functools.partial(step_kernel, n_dp, n_width, scale), out_...  39.3 us
    pallas_call x1, Pallas kernels, shards(): pl.pallas_call(hand_over, out_shape=tuple((jax.ShapeDtypeStruct(out.shape...  0.96 us

profile of v3, /device:TPU:0, one launch (start us, length us, event | category | flops | bytes accessed | tf_op | source)
XLA Modules:
  0.0 40.9 jit_solution(6050046708582105854)
XLA Ops:
  0.6 39.3 %shard_map.92 = (bf16[192,512]{1,0:T(8,128)(2,1)S(1)}, bf16[192,512]{1,0:T(8,128)(2,1)S(1)}, f32[3,64,512]{2,1,0:T(8,128)S(1)}, f32[64,256]{1,0:T(8,128)S(1)}, f32[32,512]{1,0:T(8,128)S(1)}) custom-call(bf16[192,512]{1,0:T(8,128)(2,1)} %bitcast.17, bf16[3,512,512]{2,1,0:T(8,128)(2,1)} %bitcast.14, bf16[512,256]{1,0:T(8,128)(2,1)} %bitcast.15, ...), custom_call_target="tpu_custom_call" | custom-call | tf_op jit(solution)/shard_map/pallas_call | solution.py:422
  39.9 1.0 %shard_map.93 = (bf16[192,512]{1,0:T(8,128)(2,1)}, bf16[192,512]{1,0:T(8,128)(2,1)}, f32[3,64,512]{2,1,0:T(8,128)}, f32[64,256]{1,0:T(8,128)}, f32[32,512]{1,0:T(8,128)}) custom-call(bf16[192,512]{1,0:T(8,128)(2,1)S(1)} %get-tuple-element.15.refs_0_, bf16[192,512]{1,0:T(8,128)(2,1)S(1)} %get-tuple-element.16.refs_1_, ...), custom_call_target="tpu_custom_call" | custom-call | tf_op jit(solution)/shard_map/pallas_call | solution.py:484

commit v4 on v3

--- a/solution.py
+++ b/solution.py
@@ -121,7 +121,7 @@
     x_hbm, w_hbm, left_hbm, right_hbm, g_hbm,
     act_out, in_out, block_out, left_out, right_out,
     x, w, left, right, g,
-    xs, lat_own, lat_got, lg_own, lg_got, hidden, x_t, h_t, lat_t,
+    xs, lat_sum, lat_own, lat_got, lat_full, lg_own, lg_got, hidden, x_t, h_t, lat_t,
     back_own, back_got, pre, own_back,
     main_away, main_own, main_core, main_send, main_lo, main_hi,
     low_away, low_own, low_core, low_send, low_lo, low_hi,
@@ -178,36 +178,66 @@
     pl.semaphore_wait(barrier, n_width + 2 - ends)
 
     loads[0].wait()
+    tall = x.shape[0]
+    share = tall // n_width
+    halves = [slice(0, tall // 2), slice(tall // 2, tall)]
     x_copies = [
-        remote(x, xs.at[bit], x_send.at[bit], x_recv.at[bit], dp, mate(1 << bit))
-        for bit in range(levels)
+        [
+            remote(
+                x.at[half], xs.at[bit, half], x_send.at[part, bit], x_recv.at[part, bit],
+                dp, mate(1 << bit),
+            )
+            for bit in range(levels)
+        ]
+        for part, half in enumerate(halves)
     ]
+
+    def rows_of(device):
+        return pl.ds(pl.multiple_of(device * share, share), share)
+
     loads[1].wait()
-    lat_mine = dot_nn(x[...], left[...])
-    lat_own[...] = lat_mine.astype(bf16)
+    lat_sum[...] = dot_nn(x[...], left[...])
+    lat_own[...] = lat_sum[...].astype(bf16)
     lat_copies = [
-        remote(lat_own, lat_got.at[k - 1], lat_send.at[k - 1], lat_recv.at[k - 1], dp, mate(k))
+        remote(
+            lat_own.at[rows_of(mate(k))], lat_got.at[k - 1],
+            lat_send.at[0, k - 1], lat_recv.at[0, k - 1], dp, mate(k),
+        )
         for k in range(1, n_width)
     ]
-    for copy in lat_copies:
-        copy.start()
-    for copy in x_copies:
+    for copy in lat_copies + x_copies[0]:
         copy.start()
     loads[2].wait()
     pre[...] = dot_nt(x[...], w[0])
+    for copy in lat_copies:
+        copy.wait_recv()
+    mine = lat_sum[rows_of(me), :]
+    for k in range(n_width - 1):
+        mine = mine + lat_got[k].astype(f32)
+    lat_full[rows_of(me), :] = mine.astype(bf16)
+    full_copies = [
+        remote(
+            lat_full.at[rows_of(me)], lat_full.at[rows_of(me)],
+            lat_send.at[1, k - 1], lat_recv.at[1, k - 1], dp, mate(k),
+        )
+        for k in range(1, n_width)
+    ]
+    for copy in full_copies + x_copies[1]:
+        copy.start()
     x_t[...] = x[...].astype(f32).T.astype(bf16).reshape(x_t.shape)
     loads[3].wait()
     loads[4].wait()
-    for copy in lat_copies:
-        copy.wait_recv()
-    lat_sum = lat_mine
-    for k in range(n_width - 1):
-        lat_sum = lat_sum + lat_got[k].astype(f32)
-    latent = lat_sum.astype(bf16)
-    lat_t[...] = lat_sum.T.astype(bf16).reshape(lat_t.shape)
+    for k in range(1, n_width):
+        remote(
+            lat_full.at[rows_of(mate(k))], lat_full.at[rows_of(mate(k))],
+            lat_send.at[1, k - 1], lat_recv.at[1, k - 1], dp, mate(k),
+        ).wait_recv()
+    latent = lat_full[...]
+    lat_t[...] = latent.astype(f32).T.astype(bf16).reshape(lat_t.shape)
     pre[...] += dot_nn(latent, right[...])
     for bit in range(levels):
-        x_copies[bit].wait_recv()
+        for part in range(2):
+            x_copies[part][bit].wait_recv()
         pre[...] += dot_nt(xs[bit], w[bit + 1])
 
     v = pre[...]
@@ -375,7 +405,7 @@
                 if s == levels:
                     right_out[...] = total[ob:] * scale
 
-    for copy in x_copies + lat_copies + lg_copies + back_copies:
+    for copy in x_copies[0] + x_copies[1] + lat_copies + full_copies + lg_copies + back_copies:
         copy.wait_send()
     for s in range(last + 1):
         for c in range(chips):
@@ -401,7 +431,7 @@
     width_out = block_weights.shape[1]
     rank = low_left.shape[2]
     ob, ib, rb = width_out // n_dp, width_in // n_dp, rank // n_dp
-    fits = n_dp % 2 == 0 and rows % 16 == 0 and width_in == width_out
+    fits = n_dp % 2 == 0 and rows % (16 * n_width) == 0 and rows % 32 == 0 and width_in == width_out
     if not fits or ob % 16 or ib % 16 or rb % 16 or width_in % 128 or rank % 128:
         return plain_shards(inputs, block_weights, low_left, low_right, out_grad)
     chips = n_dp // 2
@@ -437,8 +467,10 @@
             vm((rank, width_out), bf16),
             vm((rows, width_out), bf16),
             vm((levels, rows, width_in), bf16),
+            vm((rows, rank), f32),
             vm((rows, rank), bf16),
-            vm((n_width - 1, rows, rank), bf16),
+            vm((n_width - 1, rows // n_width, rank), bf16),
+            vm((rows, rank), bf16),
             vm((rows, rank), bf16),
             vm((n_width - 1, rows, rank), bf16),
             vm((rows, width_out), bf16),
@@ -452,10 +484,10 @@
             *line_scratch(main, width_in),
             *line_scratch(ib, rank),
             dma((5,)),
-            dma((levels,)),
-            dma((levels,)),
-            dma((n_width - 1,)),
-            dma((n_width - 1,)),
+            dma((2, levels)),
+            dma((2, levels)),
+            dma((2, n_width - 1)),
+            dma((2, n_width - 1)),
             dma((n_width - 1,)),
             dma((n_width - 1,)),
             dma((levels,)),

time: 41 us -> 39 us (0.951)
  Pallas kernels: 40.2 us -> 38.2 us
    pallas_call x1, Pallas kernels: 39.3 us -> 37.2 us  [shards(): pl.pallas_call(functools.partial(step_kernel, n_dp, n_width, scale), out_...]
where the time goes in v4:
time: 39 us; the launch traced here: 38.8 us
  Pallas kernels  38.2 us (98%)
  between operations  0.64 us (2%)
    pallas_call x1, Pallas kernels, shards(): pl.pallas_call(functools.partial(step_kernel, n_dp, n_width, scale), out_...  37.2 us
    pallas_call x1, Pallas kernels, shards(): pl.pallas_call(hand_over, out_shape=tuple((jax.ShapeDtypeStruct(out.shape...  0.96 us

profile of v4, /device:TPU:0, one launch (start us, length us, event | category | flops | bytes accessed | tf_op | source)
XLA Modules:
  0.0 38.8 jit_solution(10618928645749682664)
XLA Ops:
  0.6 37.2 %shard_map.92 = (bf16[192,512]{1,0:T(8,128)(2,1)S(1)}, bf16[192,512]{1,0:T(8,128)(2,1)S(1)}, f32[3,64,512]{2,1,0:T(8,128)S(1)}, f32[64,256]{1,0:T(8,128)S(1)}, f32[32,512]{1,0:T(8,128)S(1)}) custom-call(bf16[192,512]{1,0:T(8,128)(2,1)} %bitcast.17, bf16[3,512,512]{2,1,0:T(8,128)(2,1)} %bitcast.14, bf16[512,256]{1,0:T(8,128)(2,1)} %bitcast.15, ...), custom_call_target="tpu_custom_call" | custom-call | tf_op jit(solution)/shard_map/pallas_call | solution.py:452
  37.9 1.0 %shard_map.93 = (bf16[192,512]{1,0:T(8,128)(2,1)}, bf16[192,512]{1,0:T(8,128)(2,1)}, f32[3,64,512]{2,1,0:T(8,128)}, f32[64,256]{1,0:T(8,128)}, f32[32,512]{1,0:T(8,128)}) custom-call(bf16[192,512]{1,0:T(8,128)(2,1)S(1)} %get-tuple-element.15.refs_0_, bf16[192,512]{1,0:T(8,128)(2,1)S(1)} %get-tuple-element.16.refs_1_, ...), custom_call_target="tpu_custom_call" | custom-call | tf_op jit(solution)/shard_map/pallas_call | solution.py:516
